TPU v7x, 256 devices: a whole 4x4x8 slice. The times are simulated.
256 devices in a mesh: energy: 32 (over x, y, core), cell: 8 (over z).
Axes of the slice: x: 4, y: 4, z: 8, core: 2. Of those that a mesh axis runs over, the one named last changes fastest.
Arguments:
- retarded_diag: bfloat16 [2, 64, 32, 256, 256], P(None, 'energy', 'cell'), may hold values from -0.375 to 0.375
- retarded_lower: bfloat16 [2, 64, 32, 256, 256], P(None, 'energy', 'cell'), may hold values from -0.375 to 0.375
- retarded_upper: bfloat16 [2, 64, 32, 256, 256], P(None, 'energy', 'cell'), may hold values from -0.375 to 0.375
- sigma_lesser: bfloat16 [2, 64, 32, 256, 256], P(None, 'energy', 'cell'), may hold values from -6 to 6
- screened: bfloat16 [2, 32, 128], P(None, 'cell'), may hold values from -0.5 to 0.5
- kept: int32 [32, 8], P('cell'), may hold values from 0 to 15, as said below
- kept_count: int32 [32], P('cell'), may hold values from 1 to 8, as said below
Outputs:
- sigma_new: bfloat16 [2, 64, 32, 8, 4096], P(None, 'energy', 'cell')
Inputs may be any that keep to these rules, and one draw needn't show every extreme that they name: `kept`: each row holds 8 different sub-block numbers. `kept_count`: some cell has 8 live slots and some other cell 1.
All inputs are finite; a program needn't handle non-finite values.
Results may differ from a plain program's by a relative error of at most 0.0057.
Values may be sent and summed in bfloat16 or wider, within the bound.
A program may use at most 128 MiB of HBM per device.

v0:
```python
from functools import partial
import jax
import jax.numpy as jnp
from jax import lax
from jax.sharding import PartitionSpec as P

ORB = 256
SUB = 64
KMAX = 8


def with_halo(block, sides, width):
    for axis, dim in sides:
        count = lax.axis_size(axis)
        forward = [(i, i + 1) for i in range(count - 1)]
        backward = [(target, source) for source, target in forward]
        low = lax.ppermute(
            lax.slice_in_dim(block, block.shape[dim] - width, None, axis=dim), axis, forward
        )
        high = lax.ppermute(lax.slice_in_dim(block, 0, width, axis=dim), axis, backward)
        block = jnp.concatenate([low, block, high], axis=dim)
    return block


def batched(left_side, right_side):
    return jnp.einsum("ecij,ecjk->ecik", left_side, right_side, preferred_element_type=jnp.float32)


def strips(hot, blocks):
    shaped = blocks.reshape(blocks.shape[0], blocks.shape[1], hot.shape[2], SUB, blocks.shape[3])
    return jnp.einsum("ckp,ecpij->eckij", hot, shaped, preferred_element_type=jnp.float32).astype(
        jnp.bfloat16
    )


def outer_part(left_side, right_side):
    return jnp.einsum(
        "eckij,eckqj->cekiq", left_side, right_side, preferred_element_type=jnp.float32
    )


def kept_sandwich(row_hot, col_hot, factor, middle):
    inner_r = (batched(factor[0], middle[0]) - batched(factor[1], middle[1])).astype(jnp.bfloat16)
    inner_i = (batched(factor[0], middle[1]) + batched(factor[1], middle[0])).astype(jnp.bfloat16)
    rows_r = strips(row_hot, inner_r)
    rows_i = strips(row_hot, inner_i)
    factor_r = strips(col_hot, factor[0])
    factor_i = strips(col_hot, factor[1])
    outer_r = outer_part(rows_r, factor_r) + outer_part(rows_i, factor_i)
    outer_i = outer_part(rows_i, factor_r) - outer_part(rows_r, factor_i)
    return (outer_r, outer_i)


def toeplitz(screened):
    energy_count = screened.shape[2] // 2
    position = jnp.arange(energy_count, dtype=jnp.int32)
    offsets = position[:, None] - position[None, :] + energy_count - 1
    return jnp.take(screened, offsets, axis=2)


def convolve(kernel, chosen):
    shape_in = chosen.shape
    flat = chosen.reshape(2, shape_in[1], shape_in[2], shape_in[3] * shape_in[4])
    form = "cef,cfm->cem"
    real_part = jnp.einsum(
        form, kernel[0], flat[0], preferred_element_type=jnp.float32
    ) - jnp.einsum(form, kernel[1], flat[1], preferred_element_type=jnp.float32)
    imag_part = jnp.einsum(
        form, kernel[0], flat[1], preferred_element_type=jnp.float32
    ) + jnp.einsum(form, kernel[1], flat[0], preferred_element_type=jnp.float32)
    return jnp.stack([real_part, imag_part]).astype(jnp.bfloat16).reshape(shape_in)


def per_device(
    retarded_diag, retarded_lower, retarded_upper, sigma_lesser, screened, kept, kept_count
):
    padded = with_halo(sigma_lesser, (("cell", 2),), 1)
    cell_count = sigma_lesser.shape[2]
    prev_cell = padded[:, :, 0:cell_count]
    next_cell = padded[:, :, 2 : cell_count + 2]
    per_side = ORB // SUB
    sides = jnp.arange(per_side, dtype=jnp.int32)
    row_hot = ((kept // per_side)[:, :, None] == sides[None, None, :]).astype(jnp.bfloat16)
    col_hot = ((kept % per_side)[:, :, None] == sides[None, None, :]).astype(jnp.bfloat16)
    first_r, first_i = kept_sandwich(row_hot, col_hot, retarded_diag, sigma_lesser)
    second_r, second_i = kept_sandwich(row_hot, col_hot, retarded_lower, prev_cell)
    third_r, third_i = kept_sandwich(row_hot, col_hot, retarded_upper, next_cell)
    lesser = jnp.stack([first_r + second_r + third_r, first_i + second_i + third_i]).astype(
        jnp.bfloat16
    )
    lesser = lesser.reshape(lesser.shape[:4] + (SUB * SUB,))
    live_slots = (jnp.arange(KMAX, dtype=jnp.int32)[None, :] < kept_count[:, None]).astype(
        jnp.bfloat16
    )
    chosen = lesser * live_slots[None, :, None, :, None]
    kernel = toeplitz(screened)
    mapper = partial(convolve, kernel)
    convolved = mapper(lax.all_to_all(chosen, "energy", split_axis=4, concat_axis=2, tiled=True))
    result = lax.all_to_all(convolved, "energy", split_axis=2, concat_axis=4, tiled=True)
    return jnp.swapaxes(result, 1, 2)


def solution(mesh):
    placed = (
        P(None, "energy", "cell", None, None),
        P(None, "energy", "cell", None, None),
        P(None, "energy", "cell", None, None),
        P(None, "energy", "cell", None, None),
        P(None, "cell", None),
        P("cell", None),
        P("cell"),
    )
    return jax.shard_map(
        per_device,
        mesh=mesh,
        in_specs=placed,
        out_specs=P(None, "energy", "cell", None, None),
        check_vma=False,
    )
```

profile of v0, /device:TPU:129, one launch (start us, length us, event | category | flops | bytes accessed | tf_op | source)
XLA Modules:
  0.0 209.8 jit_solution(11229530620356024958)
XLA Ops:
  0.0 1.4 fusion.119
  1.4 2.6 %collective-permute-start = (bf16[2,2,1,256,256]{4,3,2,1,0:T(8,128)(2,1)S(1)}, bf16[2,2,1,256,256]{4,3,2,1,0:T(8,128)(2,1)S(1)}, u32[]{:S(2)}, u32[]{:S(2)}) collective-permute-start(bf16[2,2,1,256,256]{4,3,2,1,0:T(8,128)(2,1)S(1)} %get-tuple-element.11), channel_id=1, source_target_pairs={{0,1},{1,2},{2,3},{3,4},{4,5},{5,6},{6,7},{8,9},{9,10},{10,11},{11... | collective-permute-start | bytes 1572872 | tf_op jit(solution)/shard_map/ppermute | solution.py:17
  4.1 4.0 %collective-permute-start.1 = (bf16[2,2,1,256,256]{4,3,2,1,0:T(8,128)(2,1)S(1)}, bf16[2,2,1,256,256]{4,3,2,1,0:T(8,128)(2,1)S(1)}, u32[]{:S(2)}, u32[]{:S(2)}) collective-permute-start(bf16[2,2,1,256,256]{4,3,2,1,0:T(8,128)(2,1)S(1)} %get-tuple-element.12), channel_id=1, source_target_pairs={{1,0},{2,1},{3,2},{4,3},{5,4},{6,5},{7,6},{9,8},{10,9},{11,10},{12... | collective-permute-start | bytes 1572872 | tf_op jit(solution)/shard_map/ppermute | solution.py:20
  8.1 1.7 fusion.58
  12.7 0.9 convert_bitcast_fusion.11
  13.7 1.1 convert_bitcast_fusion.8
  14.8 1.1 convert_bitcast_fusion.10
  15.9 2.2 %fusion.24 = f32[4,2,8,64,64]{4,3,2,1,0:T(8,128)} fusion(bf16[2,4,8,64,256]{4,2,3,0,1:T(8,128)(2,1)S(1)} %convert_bitcast_fusion.8, bf16[2,4,8,64,256]{4,2,3,0,1:T(8,128)(2,1)S(1)} %convert_bitcast_fusion.11), kind=kOutput, calls=%fused_computation.45 | convolution fusion | flops 134217728 | bytes 5242880 | tf_op jit(solution)/shard_map/eckij,eckqj->cekiq/dot_general | solution.py:37
  19.9 1.1 convert_bitcast_fusion.6
  21.0 1.1 convert_bitcast_fusion.4
  22.8 1.1 convert_bitcast_fusion.2
  23.9 1.3 convert_bitcast_fusion
  27.2 0.9 convert_bitcast_fusion.3
  28.1 2.1 %fusion = f32[4,2,8,64,64]{4,3,2,1,0:T(8,128)} fusion(bf16[2,4,8,64,256]{4,2,3,0,1:T(8,128)(2,1)S(1)} %convert_bitcast_fusion, bf16[2,4,8,64,256]{4,2,3,0,1:T(8,128)(2,1)S(1)} %convert_bitcast_fusion.3), kind=kOutput, calls=%fused_computation.21 | convolution fusion | flops 134217728 | bytes 5242880 | tf_op jit(solution)/shard_map/eckij,eckqj->cekiq/dot_general | solution.py:37
  32.4 2.1 %fusion.4 = f32[4,2,8,64,64]{4,3,2,1,0:T(8,128)} fusion(bf16[2,4,8,64,256]{4,2,3,0,1:T(8,128)(2,1)S(1)} %convert_bitcast_fusion.1, bf16[2,4,8,64,256]{4,2,3,0,1:T(8,128)(2,1)S(1)} %convert_bitcast_fusion.2), kind=kOutput, calls=%fused_computation.25 | convolution fusion | flops 134217728 | bytes 5242880 | tf_op jit(solution)/shard_map/eckij,eckqj->cekiq/dot_general | solution.py:37
  36.7 0.9 convert_bitcast_fusion.7
  37.7 2.2 %fusion.12 = f32[4,2,8,64,64]{4,3,2,1,0:T(8,128)} fusion(bf16[2,4,8,64,256]{4,2,3,0,1:T(8,128)(2,1)S(1)} %convert_bitcast_fusion.4, bf16[2,4,8,64,256]{4,2,3,0,1:T(8,128)(2,1)S(1)} %convert_bitcast_fusion.7), kind=kOutput, calls=%fused_computation.33 | convolution fusion | flops 134217728 | bytes 5242880 | tf_op jit(solution)/shard_map/eckij,eckqj->cekiq/dot_general | solution.py:37
  42.0 2.4 %fusion.16 = f32[4,2,8,64,64]{4,3,2,1,0:T(8,128)} fusion(bf16[2,4,8,64,256]{4,2,3,0,1:T(8,128)(2,1)S(1)} %convert_bitcast_fusion.5, bf16[2,4,8,64,256]{4,2,3,0,1:T(8,128)(2,1)S(1)} %convert_bitcast_fusion.6), kind=kOutput, calls=%fused_computation.37 | convolution fusion | flops 134217728 | bytes 5242880 | tf_op jit(solution)/shard_map/eckij,eckqj->cekiq/dot_general | solution.py:37
  45.2 1.3 add_convert_fusion.1
  46.5 1.6 stack.18
  48.2 6.0 %add_convert_fusion = bf16[4,2,8,64,64]{4,3,2,1,0:T(8,128)(2,1)S(1)} fusion(f32[4,2,8,64,64]{4,3,2,1,0:T(8,128)} %fusion.4, f32[4,2,8,64,64]{4,3,2,1,0:T(8,128)} %fusion, f32[4,2,8,64,64]{4,3,2,1,0:T(8,128)} %fusion.16, f32[4,2,8,64,64]{4,3,2,1,0:T(8,128)} %fusion.12, f32[4,2,8,64,64]{4,3,2,1,0:T(8,128)} %fusion.24, ...), kind=kOutput, calls=%fused_computation.1 | convolution fusion | flops 135790592 | bytes 9961472 | tf_op jit(solution)/shard_map/eckij,eckqj->cekiq/dot_general | solution.py:37
  54.9 1.2 maximum_multiply_fusion
  56.1 28.1 %copy.169 = bf16[2,4,2,8,4096]{3,2,1,0,4:T(2,128)(2,1)} copy(bf16[2,4,2,8,4096]{4,3,2,1,0:T(8,128)(2,1)S(1)} %maximum_multiply_fusion) | data formatting | bytes 2097152 | tf_op jit(solution)/shard_map/mul | solution.py:95
  84.2 20.6 %reshape.121 = bf16[32,2,8192]{2,1,0:T(2,128)(2,1)} reshape(bf16[4096,2,4,2,8]{4,3,2,1,0:T(2,128)(2,1)} %bitcast.165) | data formatting | bytes 2097152
  104.8 8.5 %all-to-all-start = ((bf16[32,2,8192]{2,1,0:T(2,128)(2,1)}), bf16[32,2,8192]{2,1,0:T(2,128)(2,1)S(1)}, u32[]{:S(2)}, u32[]{:S(2)}) async-start(bf16[32,2,8192]{2,1,0:T(2,128)(2,1)} %reshape.121), calls=%async_computation | async-start | bytes 2097152 | tf_op jit(solution)/shard_map/all_to_all | solution.py:98
  113.6 13.8 %gather_fusion = bf16[4096,2,4]{2,1,0:T(2,128)(2,1)S(1)} fusion(bf16[2,4,128]{1,0,2:T(2,128)(2,1)S(1)} %copy.130, s32[4096]{0:T(1024)S(1)} %broadcast_clamp_fusion), kind=kCustom, calls=%fused_computation | custom fusion | bytes 147456 | tf_op jit(solution)/shard_map/jit(_take)/gather | solution.py:58
  127.3 1.8 copy.176
  129.2 1.0 all-to-all-done
  130.2 20.8 %reshape.122 = bf16[4096,2,4,2,8]{4,3,2,1,0:T(2,128)(2,1)} reshape(bf16[32,2,8192]{2,1,0:T(2,128)(2,1)S(1)} %all-to-all-done) | data formatting | bytes 2097152
  151.0 32.1 %copy.170 = bf16[2,4,2,8,32,128]{5,3,2,4,1,0:T(8,128)(2,1)S(1)} copy(bf16[2,4,2,8,32,128]{3,2,1,0,5,4:T(2,128)(2,1)} %bitcast.166) | data formatting | bytes 2097152 | tf_op jit(solution)/shard_map/all_to_all | solution.py:98
  185.5 23.1 %all_to_all.33 = bf16[2,4,64,8,128]{4,3,1,0,2:T(8,128)(2,1)S(1)} all-to-all(bf16[2,4,64,8,128]{4,3,1,0,2:T(8,128)(2,1)S(1)} %copy.177), channel_id=1, replica_groups=mesh['energy'=32,'cell'=8] {'energy'}, dimensions={2} | all-to-all | bytes 2097152 | tf_op jit(solution)/shard_map/all_to_all | solution.py:99
  208.6 1.2 copy.262
  (63 shorter events, 17.9 us)
Async XLA Ops:
  0.0 8.1 %copy-start = (bf16[2,2,4,256,256]{4,3,2,1,0:T(8,128)(2,1)S(1)}, bf16[2,2,4,256,256]{4,3,2,1,0:T(8,128)(2,1)}, u32[]{:S(2)}) copy-start(bf16[2,2,4,256,256]{4,3,2,1,0:T(8,128)(2,1)} %param.10) | copy-start | bytes 6291460
  1.4 23.9 %collective-permute-start = (bf16[2,2,1,256,256]{4,3,2,1,0:T(8,128)(2,1)S(1)}, bf16[2,2,1,256,256]{4,3,2,1,0:T(8,128)(2,1)S(1)}, u32[]{:S(2)}, u32[]{:S(2)}) collective-permute-start(bf16[2,2,1,256,256]{4,3,2,1,0:T(8,128)(2,1)S(1)} %get-tuple-element.11), channel_id=1, source_target_pairs={{0,1},{1,2},{2,3},{3,4},{4,5},{5,6},{6,7},{8,9},{9,10},{10,11},{11... | collective-permute-start | bytes 1572872 | tf_op jit(solution)/shard_map/ppermute | solution.py:17
  4.1 5.7 %copy-start.1 = (bf16[2,2,4,256,256]{4,3,2,1,0:T(8,128)(2,1)S(1)}, bf16[2,2,4,256,256]{4,3,2,1,0:T(8,128)(2,1)}, u32[]{:S(2)}) copy-start(bf16[2,2,4,256,256]{4,3,2,1,0:T(8,128)(2,1)} %param.7) | copy-start | bytes 6291460
  4.1 21.7 %collective-permute-start.1 = (bf16[2,2,1,256,256]{4,3,2,1,0:T(8,128)(2,1)S(1)}, bf16[2,2,1,256,256]{4,3,2,1,0:T(8,128)(2,1)S(1)}, u32[]{:S(2)}, u32[]{:S(2)}) collective-permute-start(bf16[2,2,1,256,256]{4,3,2,1,0:T(8,128)(2,1)S(1)} %get-tuple-element.12), channel_id=1, source_target_pairs={{1,0},{2,1},{3,2},{4,3},{5,4},{6,5},{7,6},{9,8},{10,9},{11,10},{12... | collective-permute-start | bytes 1572872 | tf_op jit(solution)/shard_map/ppermute | solution.py:20
  10.2 0.7 copy-start.5
  12.7 5.4 %copy-start.4 = (bf16[2,4,8,64,256]{4,2,3,0,1:T(8,128)(2,1)}, bf16[2,4,8,64,256]{4,2,3,0,1:T(8,128)(2,1)S(1)}, u32[]{:S(2)}) copy-start(bf16[2,4,8,64,256]{4,2,3,0,1:T(8,128)(2,1)S(1)} %convert_bitcast_fusion.9) | copy-start | bytes 6291460
  18.1 1.6 copy-start.3
  21.0 1.6 copy-start.2
  23.9 1.3 copy-start.7
  104.8 8.6 %copy-start.6 = (bf16[2,4,128]{2,1,0:T(4,128)(2,1)S(1)}, bf16[2,4,128]{2,1,0:T(4,128)(2,1)}, u32[]{:S(2)}) copy-start(bf16[2,4,128]{2,1,0:T(4,128)(2,1)} %param.11) | copy-start | bytes 6148
  104.8 25.4 %all-to-all-start = ((bf16[32,2,8192]{2,1,0:T(2,128)(2,1)}), bf16[32,2,8192]{2,1,0:T(2,128)(2,1)S(1)}, u32[]{:S(2)}, u32[]{:S(2)}) async-start(bf16[32,2,8192]{2,1,0:T(2,128)(2,1)} %reshape.121), calls=%async_computation | async-start | bytes 2097152 | tf_op jit(solution)/shard_map/all_to_all | solution.py:98
where the time goes:
time: 211 us; the launch traced here: 210 us
  local copies, waits for them, and re-layouts  126 us (60%)
  matrix products  42.3 us (20%)
  blocking collectives  23.1 us (11%)
  starting transfers between devices  15.1 us (7%)
    unnamed x22, local copies, waits for them, and re-layouts  43.6 us
    all_to_all x1, local copies, waits for them, and re-layouts, per_device(): lax.all_to_all(chosen, 'energy', split_axis=4, concat_axis=2, tiled=True)  32.1 us
    mul x1, local copies, waits for them, and re-layouts, per_device(): chosen = lesser * live_slots[None, :, None, :, None]  28.1 us
    all_to_all x1, blocking collectives, per_device(): lax.all_to_all(convolved, 'energy', split_axis=2, concat_axis=4, tiled=True)  23.1 us
    dot_general x12, matrix products, outer_part(): jnp.einsum('eckij,eckqj->cekiq', left_side, right_side, preferred_element...  22.3 us
    gather x2, local copies, waits for them, and re-layouts, toeplitz(): return jnp.take(screened, offsets, axis=2)  15.6 us
    dot_general x12, matrix products, strips(): jnp.einsum('ckp,ecpij->eckij', hot, shaped, preferred_element_type=jnp.fl...  12.3 us
    all_to_all x1, starting transfers between devices, per_device(): lax.all_to_all(chosen, 'energy', split_axis=4, concat_axis=2, tiled=True)  8.46 us
  transfers between devices with their start and end apart: 3, of which 1 were waited for; matrix products, arithmetic and copies ran while one was open for 15% of the time, Pallas kernels for 0%

commit v1 on v0

--- a/solution.py
+++ b/solution.py
@@ -96,7 +96,12 @@
     kernel = toeplitz(screened)
     mapper = partial(convolve, kernel)
     convolved = mapper(lax.all_to_all(chosen, "energy", split_axis=4, concat_axis=2, tiled=True))
-    result = lax.all_to_all(convolved, "energy", split_axis=2, concat_axis=4, tiled=True)
+    result = jnp.concatenate(
+        lax.all_to_all(
+            jnp.stack(jnp.split(convolved, lax.axis_size("energy"), axis=2)), "energy", 0, 0
+        ),
+        axis=4,
+    )
     return jnp.swapaxes(result, 1, 2)
 
 

time: 211 us -> 212 us (level)
    unnamed x22 -> x54, local copies, waits for them, and re-layouts: 43.6 us -> 44.1 us
where the time goes in v1:
time: 212 us; the launch traced here: 210 us
  local copies, waits for them, and re-layouts  127 us (60%)
  matrix products  42.3 us (20%)
  blocking collectives  23.1 us (11%)
  starting transfers between devices  15.1 us (7%)
    unnamed x54, local copies, waits for them, and re-layouts  44.1 us
    all_to_all x1, local copies, waits for them, and re-layouts, per_device(): lax.all_to_all(chosen, 'energy', split_axis=4, concat_axis=2, tiled=True)  32.1 us
    mul x1, local copies, waits for them, and re-layouts, per_device(): chosen = lesser * live_slots[None, :, None, :, None]  28.1 us
    all_to_all x1, blocking collectives, per_device(): lax.all_to_all(jnp.stack(jnp.split(convolved, lax.axis_size('energy'), ax...  23.1 us
    dot_general x12, matrix products, outer_part(): jnp.einsum('eckij,eckqj->cekiq', left_side, right_side, preferred_element...  22.3 us
    gather x2, local copies, waits for them, and re-layouts, toeplitz(): return jnp.take(screened, offsets, axis=2)  15.6 us
    dot_general x12, matrix products, strips(): jnp.einsum('ckp,ecpij->eckij', hot, shaped, preferred_element_type=jnp.fl...  12.3 us
    all_to_all x1, starting transfers between devices, per_device(): lax.all_to_all(chosen, 'energy', split_axis=4, concat_axis=2, tiled=True)  8.46 us
  transfers between devices with their start and end apart: 3, of which 1 were waited for; matrix products, arithmetic and copies ran while one was open for 15% of the time, Pallas kernels for 0%

profile of v1, /device:TPU:129, one launch (start us, length us, event | category | flops | bytes accessed | tf_op | source)
XLA Modules:
  0.0 210.0 jit_solution(1053324509742026319)
XLA Ops:
  0.0 1.4 fusion.119
  1.4 2.6 %collective-permute-start = (bf16[2,2,1,256,256]{4,3,2,1,0:T(8,128)(2,1)S(1)}, bf16[2,2,1,256,256]{4,3,2,1,0:T(8,128)(2,1)S(1)}, u32[]{:S(2)}, u32[]{:S(2)}) collective-permute-start(bf16[2,2,1,256,256]{4,3,2,1,0:T(8,128)(2,1)S(1)} %get-tuple-element.11), channel_id=1, source_target_pairs={{0,1},{1,2},{2,3},{3,4},{4,5},{5,6},{6,7},{8,9},{9,10},{10,11},{11... | collective-permute-start | bytes 1572872 | tf_op jit(solution)/shard_map/ppermute | solution.py:17
  4.1 4.0 %collective-permute-start.1 = (bf16[2,2,1,256,256]{4,3,2,1,0:T(8,128)(2,1)S(1)}, bf16[2,2,1,256,256]{4,3,2,1,0:T(8,128)(2,1)S(1)}, u32[]{:S(2)}, u32[]{:S(2)}) collective-permute-start(bf16[2,2,1,256,256]{4,3,2,1,0:T(8,128)(2,1)S(1)} %get-tuple-element.12), channel_id=1, source_target_pairs={{1,0},{2,1},{3,2},{4,3},{5,4},{6,5},{7,6},{9,8},{10,9},{11,10},{12... | collective-permute-start | bytes 1572872 | tf_op jit(solution)/shard_map/ppermute | solution.py:20
  8.1 1.7 fusion.58
  12.7 0.9 convert_bitcast_fusion.11
  13.7 1.1 convert_bitcast_fusion.8
  14.8 1.1 convert_bitcast_fusion.10
  15.9 2.2 %fusion.24 = f32[4,2,8,64,64]{4,3,2,1,0:T(8,128)} fusion(bf16[2,4,8,64,256]{4,2,3,0,1:T(8,128)(2,1)S(1)} %convert_bitcast_fusion.8, bf16[2,4,8,64,256]{4,2,3,0,1:T(8,128)(2,1)S(1)} %convert_bitcast_fusion.11), kind=kOutput, calls=%fused_computation.45 | convolution fusion | flops 134217728 | bytes 5242880 | tf_op jit(solution)/shard_map/eckij,eckqj->cekiq/dot_general | solution.py:37
  19.9 1.1 convert_bitcast_fusion.6
  21.0 1.1 convert_bitcast_fusion.4
  22.8 1.1 convert_bitcast_fusion.2
  23.9 1.3 convert_bitcast_fusion
  27.2 0.9 convert_bitcast_fusion.3
  28.1 2.1 %fusion = f32[4,2,8,64,64]{4,3,2,1,0:T(8,128)} fusion(bf16[2,4,8,64,256]{4,2,3,0,1:T(8,128)(2,1)S(1)} %convert_bitcast_fusion, bf16[2,4,8,64,256]{4,2,3,0,1:T(8,128)(2,1)S(1)} %convert_bitcast_fusion.3), kind=kOutput, calls=%fused_computation.21 | convolution fusion | flops 134217728 | bytes 5242880 | tf_op jit(solution)/shard_map/eckij,eckqj->cekiq/dot_general | solution.py:37
  32.4 2.1 %fusion.4 = f32[4,2,8,64,64]{4,3,2,1,0:T(8,128)} fusion(bf16[2,4,8,64,256]{4,2,3,0,1:T(8,128)(2,1)S(1)} %convert_bitcast_fusion.1, bf16[2,4,8,64,256]{4,2,3,0,1:T(8,128)(2,1)S(1)} %convert_bitcast_fusion.2), kind=kOutput, calls=%fused_computation.25 | convolution fusion | flops 134217728 | bytes 5242880 | tf_op jit(solution)/shard_map/eckij,eckqj->cekiq/dot_general | solution.py:37
  36.7 0.9 convert_bitcast_fusion.7
  37.7 2.2 %fusion.12 = f32[4,2,8,64,64]{4,3,2,1,0:T(8,128)} fusion(bf16[2,4,8,64,256]{4,2,3,0,1:T(8,128)(2,1)S(1)} %convert_bitcast_fusion.4, bf16[2,4,8,64,256]{4,2,3,0,1:T(8,128)(2,1)S(1)} %convert_bitcast_fusion.7), kind=kOutput, calls=%fused_computation.33 | convolution fusion | flops 134217728 | bytes 5242880 | tf_op jit(solution)/shard_map/eckij,eckqj->cekiq/dot_general | solution.py:37
  42.0 2.4 %fusion.16 = f32[4,2,8,64,64]{4,3,2,1,0:T(8,128)} fusion(bf16[2,4,8,64,256]{4,2,3,0,1:T(8,128)(2,1)S(1)} %convert_bitcast_fusion.5, bf16[2,4,8,64,256]{4,2,3,0,1:T(8,128)(2,1)S(1)} %convert_bitcast_fusion.6), kind=kOutput, calls=%fused_computation.37 | convolution fusion | flops 134217728 | bytes 5242880 | tf_op jit(solution)/shard_map/eckij,eckqj->cekiq/dot_general | solution.py:37
  45.2 1.3 add_convert_fusion.1
  46.5 1.6 stack.117
  48.2 6.0 %add_convert_fusion = bf16[4,2,8,64,64]{4,3,2,1,0:T(8,128)(2,1)S(1)} fusion(f32[4,2,8,64,64]{4,3,2,1,0:T(8,128)} %fusion.4, f32[4,2,8,64,64]{4,3,2,1,0:T(8,128)} %fusion, f32[4,2,8,64,64]{4,3,2,1,0:T(8,128)} %fusion.16, f32[4,2,8,64,64]{4,3,2,1,0:T(8,128)} %fusion.12, f32[4,2,8,64,64]{4,3,2,1,0:T(8,128)} %fusion.24, ...), kind=kOutput, calls=%fused_computation.1 | convolution fusion | flops 135790592 | bytes 9961472 | tf_op jit(solution)/shard_map/eckij,eckqj->cekiq/dot_general | solution.py:37
  54.9 1.2 maximum_multiply_fusion
  56.1 28.1 %copy.167 = bf16[2,4,2,8,4096]{3,2,1,0,4:T(2,128)(2,1)} copy(bf16[2,4,2,8,4096]{4,3,2,1,0:T(8,128)(2,1)S(1)} %maximum_multiply_fusion) | data formatting | bytes 2097152 | tf_op jit(solution)/shard_map/mul | solution.py:95
  84.2 20.6 %reshape.129 = bf16[32,2,8192]{2,1,0:T(2,128)(2,1)} reshape(bf16[4096,2,4,2,8]{4,3,2,1,0:T(2,128)(2,1)} %bitcast.292) | data formatting | bytes 2097152
  104.8 8.5 %all-to-all-start = ((bf16[32,2,8192]{2,1,0:T(2,128)(2,1)}), bf16[32,2,8192]{2,1,0:T(2,128)(2,1)S(1)}, u32[]{:S(2)}, u32[]{:S(2)}) async-start(bf16[32,2,8192]{2,1,0:T(2,128)(2,1)} %reshape.129), calls=%async_computation | async-start | bytes 2097152 | tf_op jit(solution)/shard_map/all_to_all | solution.py:98
  113.6 13.8 %gather_fusion = bf16[4096,2,4]{2,1,0:T(2,128)(2,1)S(1)} fusion(bf16[2,4,128]{1,0,2:T(2,128)(2,1)S(1)} %copy.128, s32[4096]{0:T(1024)S(1)} %broadcast_clamp_fusion), kind=kCustom, calls=%fused_computation | custom fusion | bytes 147456 | tf_op jit(solution)/shard_map/jit(_take)/gather | solution.py:58
  127.3 1.8 copy.172
  129.2 1.0 all-to-all-done
  130.2 20.8 %reshape.130 = bf16[4096,2,4,2,8]{4,3,2,1,0:T(2,128)(2,1)} reshape(bf16[32,2,8192]{2,1,0:T(2,128)(2,1)S(1)} %all-to-all-done) | data formatting | bytes 2097152
  151.0 32.1 %copy.168 = bf16[2,4,2,8,32,128]{5,3,2,4,1,0:T(8,128)(2,1)S(1)} copy(bf16[2,4,2,8,32,128]{3,2,1,0,5,4:T(2,128)(2,1)} %bitcast.293) | data formatting | bytes 2097152 | tf_op jit(solution)/shard_map/all_to_all | solution.py:98
  185.8 23.1 %all_to_all.20 = bf16[32,2,4,2,8,128]{5,4,3,2,1,0:T(8,128)(2,1)S(1)} all-to-all(bf16[32,2,4,2,8,128]{5,4,3,2,1,0:T(8,128)(2,1)S(1)} %constant_dynamic-update-slice_fusion.6), channel_id=1, replica_groups=mesh['energy'=32,'cell'=8] {'energy'}, dimensions={0} | all-to-all | bytes 2097152 | tf_op jit(solution)/shard_map/all_to_all | solution.py:100
  208.9 1.1 copy_bitcast_fusion
  (95 shorter events, 18.1 us)
Async XLA Ops:
  0.0 8.1 %copy-start = (bf16[2,2,4,256,256]{4,3,2,1,0:T(8,128)(2,1)S(1)}, bf16[2,2,4,256,256]{4,3,2,1,0:T(8,128)(2,1)}, u32[]{:S(2)}) copy-start(bf16[2,2,4,256,256]{4,3,2,1,0:T(8,128)(2,1)} %param.10) | copy-start | bytes 6291460
  1.4 23.9 %collective-permute-start = (bf16[2,2,1,256,256]{4,3,2,1,0:T(8,128)(2,1)S(1)}, bf16[2,2,1,256,256]{4,3,2,1,0:T(8,128)(2,1)S(1)}, u32[]{:S(2)}, u32[]{:S(2)}) collective-permute-start(bf16[2,2,1,256,256]{4,3,2,1,0:T(8,128)(2,1)S(1)} %get-tuple-element.11), channel_id=1, source_target_pairs={{0,1},{1,2},{2,3},{3,4},{4,5},{5,6},{6,7},{8,9},{9,10},{10,11},{11... | collective-permute-start | bytes 1572872 | tf_op jit(solution)/shard_map/ppermute | solution.py:17
  4.1 5.7 %copy-start.1 = (bf16[2,2,4,256,256]{4,3,2,1,0:T(8,128)(2,1)S(1)}, bf16[2,2,4,256,256]{4,3,2,1,0:T(8,128)(2,1)}, u32[]{:S(2)}) copy-start(bf16[2,2,4,256,256]{4,3,2,1,0:T(8,128)(2,1)} %param.7) | copy-start | bytes 6291460
  4.1 21.7 %collective-permute-start.1 = (bf16[2,2,1,256,256]{4,3,2,1,0:T(8,128)(2,1)S(1)}, bf16[2,2,1,256,256]{4,3,2,1,0:T(8,128)(2,1)S(1)}, u32[]{:S(2)}, u32[]{:S(2)}) collective-permute-start(bf16[2,2,1,256,256]{4,3,2,1,0:T(8,128)(2,1)S(1)} %get-tuple-element.12), channel_id=1, source_target_pairs={{1,0},{2,1},{3,2},{4,3},{5,4},{6,5},{7,6},{9,8},{10,9},{11,10},{12... | collective-permute-start | bytes 1572872 | tf_op jit(solution)/shard_map/ppermute | solution.py:20
  10.2 0.7 copy-start.5
  12.7 5.4 %copy-start.4 = (bf16[2,4,8,64,256]{4,2,3,0,1:T(8,128)(2,1)}, bf16[2,4,8,64,256]{4,2,3,0,1:T(8,128)(2,1)S(1)}, u32[]{:S(2)}) copy-start(bf16[2,4,8,64,256]{4,2,3,0,1:T(8,128)(2,1)S(1)} %convert_bitcast_fusion.9) | copy-start | bytes 6291460
  18.1 1.6 copy-start.3
  21.0 1.6 copy-start.2
  23.9 1.3 copy-start.7
  104.8 8.6 %copy-start.6 = (bf16[2,4,128]{2,1,0:T(4,128)(2,1)S(1)}, bf16[2,4,128]{2,1,0:T(4,128)(2,1)}, u32[]{:S(2)}) copy-start(bf16[2,4,128]{2,1,0:T(4,128)(2,1)} %param.11) | copy-start | bytes 6148
  104.8 25.4 %all-to-all-start = ((bf16[32,2,8192]{2,1,0:T(2,128)(2,1)}), bf16[32,2,8192]{2,1,0:T(2,128)(2,1)S(1)}, u32[]{:S(2)}, u32[]{:S(2)}) async-start(bf16[32,2,8192]{2,1,0:T(2,128)(2,1)} %reshape.129), calls=%async_computation | async-start | bytes 2097152 | tf_op jit(solution)/shard_map/all_to_all | solution.py:98
